TPU v7x, 32 devices: a whole 2x2x4 slice. The times are simulated.
32 devices in a mesh: row: 4 (over z), col: 8 (over y, x, core).
Axes of the slice: x: 2, y: 2, z: 4, core: 2. Of those that a mesh axis runs over, the one named last changes fastest.
Arguments:
- gaussian_sketch: bfloat16 [16384, 256], P(('col', 'row')), may hold values from -6 to 6
- block_values: bfloat16 [8192, 128, 128], P(('row', 'col')), may hold values from -6 to 6
- block_rows: int32 [8192], P(('row', 'col')), may hold values from 0 to 127, as said below
- block_columns: int32 [8192], P(('row', 'col')), may hold values from 0 to 127, as said below
Outputs:
- range_basis: float32 [16384, 256], P(('row', 'col'))
- upper_factor: float32 [256, 256], replicated
Inputs may be any that keep to these rules, and one draw needn't show every extreme that they name: `block_rows`: entry k * 256 + m, k = i * 8 + j, names a block row in [i * 32, (i + 1) * 32); no (row, column) pair is named twice. `block_columns`: entry k * 256 + m, k = i * 8 + j, names a block column in [j * 16, (j + 1) * 16).
All inputs are finite; a program needn't handle non-finite values.
Results may differ from a plain program's by a relative error of at most 0.0003.
Values may be sent and summed in bfloat16 or wider, within the bound.
No kernel may reach another device: no remote copies, remote signals or barrier semaphores. Data moves between devices by JAX's collectives and lax.ppermute only.
A program may use at most 128 MiB of HBM per device.

v0:
```python
import math
import jax
import jax.numpy as jnp
from jax import lax
from jax.sharding import PartitionSpec as P

PANEL = 128


def upper_parts(gram):
    lower_factor = jnp.linalg.cholesky(gram)
    identity = jnp.eye(gram.shape[0], dtype=gram.dtype)
    inverse = lax.linalg.triangular_solve(lower_factor, identity, left_side=True, lower=True)
    return (lower_factor.T, inverse.T)


def tile_product(sketch_blocks, block_values, local_rows, local_cols, tile_rows):
    group_size = math.gcd(block_values.shape[0], 64)
    col_width = sketch_blocks.shape[2]

    def advance(counter, summed):
        offset = (counter * group_size).astype(jnp.int32)
        values = lax.dynamic_slice_in_dim(block_values, offset, group_size, 0)
        row_ids = lax.dynamic_slice_in_dim(local_rows, offset, group_size, 0)
        col_ids = lax.dynamic_slice_in_dim(local_cols, offset, group_size, 0)
        picked = jnp.take(sketch_blocks, col_ids, axis=0)
        product = jnp.einsum("gab,gbs->gas", values, picked, preferred_element_type=jnp.float32)
        return summed.at[row_ids].add(product)

    initial = jnp.zeros((tile_rows, block_values.shape[1], col_width), jnp.float32)
    summed = lax.fori_loop(0, block_values.shape[0] // group_size, advance, initial)
    return summed.reshape(tile_rows * block_values.shape[1], col_width)


def on_device(gaussian_sketch, block_values, block_rows, block_columns):
    high = lax.Precision.HIGHEST
    size_row = lax.axis_size("row")
    size_col = lax.axis_size("col")
    shard_rows = gaussian_sketch.shape[0]
    block_size = block_values.shape[1]
    grid_rows = shard_rows * size_col // block_size
    grid_cols = shard_rows * size_row // block_size
    local_rows = block_rows - lax.axis_index("row") * grid_rows
    local_cols = block_columns - lax.axis_index("col") * grid_cols
    gathered = lax.all_gather(gaussian_sketch, "row", axis=0, tiled=True)
    sketch_blocks = gathered.reshape(grid_cols, block_size, gathered.shape[1])
    partial_value = tile_product(sketch_blocks, block_values, local_rows, local_cols, grid_rows)
    sketched = lax.psum_scatter(partial_value, "col", scatter_dimension=0, tiled=True)
    first_part = sketched[:, :PANEL]
    second_part = sketched[:, PANEL:]
    order_total = shard_rows * size_row * size_col
    gram_one = (
        lax.psum(jnp.dot(first_part.T, first_part, precision=high), ("row", "col")) / order_total
    )
    upper_one, inverse_one = upper_parts(gram_one)
    basis_one = jnp.dot(first_part, inverse_one, precision=high)
    coupling = (
        lax.psum(jnp.dot(basis_one.T, second_part, precision=high), ("row", "col")) / order_total
    )
    remainder = second_part - jnp.dot(basis_one, coupling, precision=high)
    gram_two = (
        lax.psum(jnp.dot(remainder.T, remainder, precision=high), ("row", "col")) / order_total
    )
    upper_two, inverse_two = upper_parts(gram_two)
    basis_two = jnp.dot(remainder, inverse_two, precision=high)
    range_basis = jnp.concatenate([basis_one, basis_two], axis=1)
    top_rows = jnp.concatenate([upper_one, coupling], axis=1)
    bottom_rows = jnp.concatenate([jnp.zeros_like(upper_two), upper_two], axis=1)
    upper_factor = jnp.concatenate([top_rows, bottom_rows], axis=0)
    return (range_basis, upper_factor)


def solution(mesh):
    return jax.shard_map(
        on_device,
        mesh=mesh,
        in_specs=(
            P(("col", "row"), None),
            P(("row", "col"), None, None),
            P(("row", "col")),
            P(("row", "col")),
        ),
        out_specs=(P(("row", "col"), None), P()),
        check_vma=False,
    )
```

profile of v0, /device:TPU:1, one launch (start us, length us, event | category | flops | bytes accessed | tf_op | source)
XLA Modules:
  0.0 643.8 jit_solution(3256187784970648376)
XLA Ops:
  7.2 0.7 all-gather.2.cloned.1.call-update
  8.0 0.7 broadcast_subtract_fusion
  8.7 30.8 %all-gather.2.cloned.1.call-done = bf16[2048,256]{1,0:T(8,128)(2,1)} async-done(((bf16[512,256]{1,0:T(8,128)(2,1)}), bf16[2048,256]{1,0:T(8,128)(2,1)}) %all-gather.2.cloned.1.call-update) | async-done | bytes 1048592 | tf_op jit(solution)/shard_map/all_gather | solution.py:45
  39.5 2.5 broadcast_in_dim.36
  41.9 118.3 %while.13 = (s32[]{:T(128)}, f32[32,128,256]{2,1,0:T(8,128)}, s32[256]{0:T(256)S(1)}, bf16[256,128,128]{2,1,0:T(8,128)(2,1)}, s32[256]{0:T(256)S(1)}, /*index=5*...) while((s32[]{:T(128)}, f32[32,128,256]{2,1,0:T(8,128)}, s32[256]{0:T(256)S(1)}, ...), condition=%wide.region_2.3_spmd, body=%wide.region_0.2_spmd.sunk | while | flops 541066816 | bytes 48240672 | solution.py:31
  41.9 0.1 compare_and_fusion.2
  42.0 2.8 gather_fusion
  44.8 7.4 %fusion.38 = f32[64,128,256]{2,1,0:T(8,128)} fusion(bf16[64,128,256]{2,1,0:T(8,128)(2,1)} %gather_fusion, pred[64]{0:T(512)(128)(4,1)S(1)} %get-tuple-element.176, bf16[256,128,128]{2,1,0:T(8,128)(2,1)} %get-tuple-element.200, s32[]{:T(128)S(6)} %select_n.59), kind=kOutput, calls=%fused_computation.2.clone.1 | convolution fusion | flops 538968064 | bytes 14680132 | tf_op jit(solution)/shard_map/while/body/eval_jaxpr/gab,gbs->gas/dot_general | solution.py:27
  52.3 19.2 %scatter_fusion = f32[32,128,256]{2,1,0:T(8,128)} fusion(f32[32,128,256]{2,1,0:T(8,128)} %get-tuple-element.188, s32[64]{0:T(128)S(1)} %compare_select_fusion.4, f32[64,128,256]{2,1,0:T(8,128)} %fusion.38), kind=kCustom, calls=%fused_computation.1.clone.1 | custom fusion | flops 2097152 | bytes 25166080 | tf_op jit(solution)/shard_map/while/body/eval_jaxpr/scatter-add | solution.py:28
  71.5 2.8 gather_fusion
  74.3 7.4 %fusion.38 = f32[64,128,256]{2,1,0:T(8,128)} fusion(bf16[64,128,256]{2,1,0:T(8,128)(2,1)} %gather_fusion, pred[64]{0:T(512)(128)(4,1)S(1)} %get-tuple-element.176, bf16[256,128,128]{2,1,0:T(8,128)(2,1)} %get-tuple-element.200, s32[]{:T(128)S(6)} %select_n.59), kind=kOutput, calls=%fused_computation.2.clone.1 | convolution fusion | flops 538968064 | bytes 14680132 | tf_op jit(solution)/shard_map/while/body/eval_jaxpr/gab,gbs->gas/dot_general | solution.py:27
  81.7 19.1 %scatter_fusion = f32[32,128,256]{2,1,0:T(8,128)} fusion(f32[32,128,256]{2,1,0:T(8,128)} %get-tuple-element.188, s32[64]{0:T(128)S(1)} %compare_select_fusion.4, f32[64,128,256]{2,1,0:T(8,128)} %fusion.38), kind=kCustom, calls=%fused_computation.1.clone.1 | custom fusion | flops 2097152 | bytes 25166080 | tf_op jit(solution)/shard_map/while/body/eval_jaxpr/scatter-add | solution.py:28
  101.0 2.8 gather_fusion
  103.7 7.4 %fusion.38 = f32[64,128,256]{2,1,0:T(8,128)} fusion(bf16[64,128,256]{2,1,0:T(8,128)(2,1)} %gather_fusion, pred[64]{0:T(512)(128)(4,1)S(1)} %get-tuple-element.176, bf16[256,128,128]{2,1,0:T(8,128)(2,1)} %get-tuple-element.200, s32[]{:T(128)S(6)} %select_n.59), kind=kOutput, calls=%fused_computation.2.clone.1 | convolution fusion | flops 538968064 | bytes 14680132 | tf_op jit(solution)/shard_map/while/body/eval_jaxpr/gab,gbs->gas/dot_general | solution.py:27
  111.2 19.6 %scatter_fusion = f32[32,128,256]{2,1,0:T(8,128)} fusion(f32[32,128,256]{2,1,0:T(8,128)} %get-tuple-element.188, s32[64]{0:T(128)S(1)} %compare_select_fusion.4, f32[64,128,256]{2,1,0:T(8,128)} %fusion.38), kind=kCustom, calls=%fused_computation.1.clone.1 | custom fusion | flops 2097152 | bytes 25166080 | tf_op jit(solution)/shard_map/while/body/eval_jaxpr/scatter-add | solution.py:28
  130.9 2.8 gather_fusion
  133.6 7.4 %fusion.38 = f32[64,128,256]{2,1,0:T(8,128)} fusion(bf16[64,128,256]{2,1,0:T(8,128)(2,1)} %gather_fusion, pred[64]{0:T(512)(128)(4,1)S(1)} %get-tuple-element.176, bf16[256,128,128]{2,1,0:T(8,128)(2,1)} %get-tuple-element.200, s32[]{:T(128)S(6)} %select_n.59), kind=kOutput, calls=%fused_computation.2.clone.1 | convolution fusion | flops 538968064 | bytes 14680132 | tf_op jit(solution)/shard_map/while/body/eval_jaxpr/gab,gbs->gas/dot_general | solution.py:27
  141.1 19.2 %scatter_fusion = f32[32,128,256]{2,1,0:T(8,128)} fusion(f32[32,128,256]{2,1,0:T(8,128)} %get-tuple-element.188, s32[64]{0:T(128)S(1)} %compare_select_fusion.4, f32[64,128,256]{2,1,0:T(8,128)} %fusion.38), kind=kCustom, calls=%fused_computation.1.clone.1 | custom fusion | flops 2097152 | bytes 25166080 | tf_op jit(solution)/shard_map/while/body/eval_jaxpr/scatter-add | solution.py:28
  160.3 50.9 %reduce-scatter.2.cloned.1.call-done = f32[512,256]{1,0:T(8,128)} async-done(((f32[4096,256]{1,0:T(8,128)}), f32[512,256]{1,0:T(8,128)}) %reduce-scatter.2.cloned.1.call-update) | async-done | bytes 524304 | tf_op jit(solution)/shard_map/reduce_scatter | solution.py:48
  211.2 2.2 fusion.11
  213.6 124.1 %all-reduce.5.cloned.1.call-done = f32[128,128]{0,1:T(8,128)} async-done(((f32[128,128]{0,1:T(8,128)}), f32[128,128]{0,1:T(8,128)}) %all-reduce.5.cloned.1.call-update) | async-done | bytes 65552 | tf_op jit(solution)/shard_map/psum | solution.py:53
  337.7 0.8 broadcast_multiply_fusion.2
  338.5 0.1 copy.7
  338.6 0.9 fusion.20
  339.5 11.7 %cholesky.44 = f32[128,128]{1,0:T(8,128)S(1)} custom-call(f32[128,128]{1,0:T(8,128)S(1)} %fusion.20), custom_call_target="Cholesky" | custom-call | tf_op jit(solution)/shard_map/jit(cholesky)/cholesky | solution.py:11
  351.2 0.6 compare_reduce_fusion.1
  351.8 0.7 fusion.22
  352.5 9.8 %custom-call.6 = f32[1,128,128]{1,2,0:T(8,128)S(1)} custom-call(f32[1,128,128]{2,1,0:T(8,128)S(1)} %get-tuple-element.131), custom_call_target="InvertDiagBlocksLowerTriangular" | custom-call | tf_op jit(solution)/shard_map/triangular_solve/custom-call.0 | solution.py:13
  362.3 0.3 fusion.15
  362.6 1.3 fusion.9
  364.0 2.2 fusion.7
  366.2 0.2 all-reduce.9.cloned.1.call-start
  366.4 118.3 %all-reduce.7.cloned.1.call-done = f32[128,128]{0,1:T(8,128)} async-done(((f32[128,128]{0,1:T(8,128)}), f32[128,128]{0,1:T(8,128)}) %all-reduce.7.cloned.1.call-update) | async-done | bytes 65552 | tf_op jit(solution)/shard_map/psum | solution.py:58
  484.7 1.6 convolution_subtract_fusion
  486.3 1.2 fusion.24
  487.5 0.8 broadcast_multiply_fusion.1
  488.3 121.6 %all-reduce.9.cloned.1.call-done = f32[128,128]{0,1:T(8,128)} async-done(((f32[128,128]{0,1:T(8,128)}), f32[128,128]{0,1:T(8,128)}) %all-reduce.9.cloned.1.call-update) | async-done | bytes 65552 | tf_op jit(solution)/shard_map/psum | solution.py:62
  610.0 0.8 broadcast_multiply_fusion
  610.8 0.1 copy.10
  610.9 0.9 fusion.18
  611.8 11.7 %cholesky.55 = f32[128,128]{1,0:T(8,128)S(1)} custom-call(f32[128,128]{1,0:T(8,128)S(1)} %fusion.18), custom_call_target="Cholesky" | custom-call | tf_op jit(solution)/shard_map/jit(cholesky)/cholesky | solution.py:11
  623.5 0.6 compare_reduce_fusion
  624.2 0.7 fusion.23
  624.8 0.8 copy.12
  625.7 9.8 %custom-call.7 = f32[1,128,128]{1,2,0:T(8,128)S(1)} custom-call(f32[1,128,128]{2,1,0:T(8,128)S(1)} %get-tuple-element.133), custom_call_target="InvertDiagBlocksLowerTriangular" | custom-call | tf_op jit(solution)/shard_map/triangular_solve/custom-call.0 | solution.py:13
  635.5 0.3 fusion.13
  635.8 0.4 fusion.25
  636.2 1.0 copy.11
  (25 shorter events, 0.9 us)
Async XLA Ops:
  7.2 32.3 %all-gather.2.cloned.1.call-start = ((), (), s32[]{:S(2)}) async-start(), calls=%async_computation.1 | async-start | bytes 1310720 | tf_op jit(solution)/shard_map/all_gather | solution.py:45
  7.9 203.3 %reduce-scatter.2.cloned.1.call-start = ((), (), s32[]{:S(2)}) async-start(), calls=%async_computation.2 | async-start | bytes 4718592 | tf_op jit(solution)/shard_map/reduce_scatter | solution.py:48
  39.5 2.5 copy-start
  160.3 177.4 %all-reduce.5.cloned.1.call-start = ((), (), s32[]{:S(2)}) async-start(), calls=%async_computation.3 | async-start | bytes 131072 | tf_op jit(solution)/shard_map/psum | solution.py:53
  213.5 271.2 %all-reduce.7.cloned.1.call-start = ((), (), s32[]{:S(2)}) async-start(), calls=%async_computation.4 | async-start | bytes 131072 | tf_op jit(solution)/shard_map/psum | solution.py:58
  366.2 243.8 %all-reduce.9.cloned.1.call-start = ((), (), s32[]{:S(2)}) async-start(), calls=%async_computation.5 | async-start | bytes 131072 | tf_op jit(solution)/shard_map/psum | solution.py:62
Sparse Core Ops, SparseCore 0:
  9.6 29.8 all-gather.1
  160.4 50.7 reduce-scatter.1
  218.3 119.2 all-reduce.4
  366.3 118.3 all-reduce.6
  491.6 118.3 all-reduce.8
where the time goes:
time: 644 us
  waiting for transfers between devices  446 us (69%)
  other arithmetic  128 us (20%)
  matrix products  39 us (6%)
  local copies, waits for them, and re-layouts  15.6 us (2%)
  between operations  13.9 us (2%)
    psum x1, waiting for transfers between devices, on_device(): lax.psum(jnp.dot(first_part.T, first_part, precision=high), ('row', 'col'))  124 us
    psum x1, waiting for transfers between devices, on_device(): lax.psum(jnp.dot(remainder.T, remainder, precision=high), ('row', 'col'))  122 us
    psum x1, waiting for transfers between devices, on_device(): lax.psum(jnp.dot(basis_one.T, second_part, precision=high), ('row', 'col'))  118 us
    scatter-add x4, other arithmetic, advance(): return summed.at[row_ids].add(product)  77.1 us
    reduce_scatter x1, waiting for transfers between devices, on_device(): lax.psum_scatter(partial_value, 'col', scatter_dimension=0, tiled=True)  50.9 us
    all_gather x1, waiting for transfers between devices, on_device(): gathered = lax.all_gather(gaussian_sketch, 'row', axis=0, tiled=True)  30.8 us
    dot_general x4, matrix products, advance(): jnp.einsum('gab,gbs->gas', values, picked, preferred_element_type=jnp.flo...  29.5 us
    another operation x6, other arithmetic, upper_parts(): lower_factor = jnp.linalg.cholesky(gram)  24.8 us
  transfers between devices with their start and end apart: 5, of which 5 were waited for; matrix products, arithmetic and copies ran while one was open for 0% of the time, Pallas kernels for 0%

commit v1 on v0

--- a/solution.py
+++ b/solution.py
@@ -5,6 +5,10 @@
 from jax.sharding import PartitionSpec as P
 
 PANEL = 128
+
+
+def reach_cells(z_in):
+    return jnp.sum(jax.lax.all_gather(z_in, ("row", "col")), axis=0)
 
 
 def upper_parts(gram):
@@ -54,9 +58,7 @@
     )
     upper_one, inverse_one = upper_parts(gram_one)
     basis_one = jnp.dot(first_part, inverse_one, precision=high)
-    coupling = (
-        lax.psum(jnp.dot(basis_one.T, second_part, precision=high), ("row", "col")) / order_total
-    )
+    coupling = reach_cells(jnp.dot(basis_one.T, second_part, precision=high)) / order_total
     remainder = second_part - jnp.dot(basis_one, coupling, precision=high)
     gram_two = (
         lax.psum(jnp.dot(remainder.T, remainder, precision=high), ("row", "col")) / order_total

time: 644 us -> 581 us (0.902)
  waiting for transfers between devices: 446 us -> 383 us
    psum x1 -> x0, waiting for transfers between devices: 118 us -> none  [on_device(): lax.psum(jnp.dot(basis_one.T, second_part, precision=high), ('row', 'col'))]
    all_gather x0 -> x1, waiting for transfers between devices: none -> 55.8 us  [reach_cells(): return jnp.sum(jax.lax.all_gather(z_in, ('row', 'col')), axis=0)]
where the time goes in v1:
time: 581 us; the launch traced here: 580 us
  waiting for transfers between devices  383 us (66%)
  other arithmetic  129 us (22%)
  matrix products  37.9 us (7%)
  local copies, waits for them, and re-layouts  15.7 us (3%)
  between operations  13.9 us (2%)
    psum x1, waiting for transfers between devices, on_device(): lax.psum(jnp.dot(first_part.T, first_part, precision=high), ('row', 'col'))  124 us
    psum x1, waiting for transfers between devices, on_device(): lax.psum(jnp.dot(remainder.T, remainder, precision=high), ('row', 'col'))  121 us
    scatter-add x4, other arithmetic, advance(): return summed.at[row_ids].add(product)  77.1 us
    all_gather x1, waiting for transfers between devices, reach_cells(): return jnp.sum(jax.lax.all_gather(z_in, ('row', 'col')), axis=0)  55.8 us
    reduce_scatter x1, waiting for transfers between devices, on_device(): lax.psum_scatter(partial_value, 'col', scatter_dimension=0, tiled=True)  50.9 us
    all_gather x1, waiting for transfers between devices, on_device(): gathered = lax.all_gather(gaussian_sketch, 'row', axis=0, tiled=True)  30.8 us
    dot_general x4, matrix products, advance(): jnp.einsum('gab,gbs->gas', values, picked, preferred_element_type=jnp.flo...  29.5 us
    another operation x6, other arithmetic, upper_parts(): lower_factor = jnp.linalg.cholesky(gram)  24.8 us
  transfers between devices with their start and end apart: 5, of which 5 were waited for; matrix products, arithmetic and copies ran while one was open for 0% of the time, Pallas kernels for 0%

profile of v1, /device:TPU:1, one launch (start us, length us, event | category | flops | bytes accessed | tf_op | source)
XLA Modules:
  0.0 580.4 jit_solution(9916369695502082556)
XLA Ops:
  7.2 0.7 all-gather.4.cloned.1.call-update
  8.0 0.7 broadcast_subtract_fusion
  8.7 30.8 %all-gather.4.cloned.1.call-done = bf16[2048,256]{1,0:T(8,128)(2,1)} async-done(((bf16[512,256]{1,0:T(8,128)(2,1)}), bf16[2048,256]{1,0:T(8,128)(2,1)}) %all-gather.4.cloned.1.call-update) | async-done | bytes 1048592 | tf_op jit(solution)/shard_map/all_gather | solution.py:49
  39.5 2.5 broadcast_in_dim.36
  41.9 118.3 %while.13 = (s32[]{:T(128)}, f32[32,128,256]{2,1,0:T(8,128)}, s32[256]{0:T(256)S(1)}, bf16[256,128,128]{2,1,0:T(8,128)(2,1)}, s32[256]{0:T(256)S(1)}, /*index=5*...) while((s32[]{:T(128)}, f32[32,128,256]{2,1,0:T(8,128)}, s32[256]{0:T(256)S(1)}, ...), condition=%wide.region_2.3_spmd, body=%wide.region_0.2_spmd.sunk | while | flops 541066816 | bytes 48240672 | solution.py:35
  42.0 2.8 gather_fusion
  44.8 7.4 %fusion.38 = f32[64,128,256]{2,1,0:T(8,128)} fusion(bf16[64,128,256]{2,1,0:T(8,128)(2,1)} %gather_fusion, pred[64]{0:T(512)(128)(4,1)S(1)} %get-tuple-element.178, bf16[256,128,128]{2,1,0:T(8,128)(2,1)} %get-tuple-element.202, s32[]{:T(128)S(6)} %select_n.59), kind=kOutput, calls=%fused_computation.2.clone.1 | convolution fusion | flops 538968064 | bytes 14680132 | tf_op jit(solution)/shard_map/while/body/eval_jaxpr/gab,gbs->gas/dot_general | solution.py:31
  52.3 19.2 %scatter_fusion = f32[32,128,256]{2,1,0:T(8,128)} fusion(f32[32,128,256]{2,1,0:T(8,128)} %get-tuple-element.190, s32[64]{0:T(128)S(1)} %compare_select_fusion.4, f32[64,128,256]{2,1,0:T(8,128)} %fusion.38), kind=kCustom, calls=%fused_computation.1.clone.1 | custom fusion | flops 2097152 | bytes 25166080 | tf_op jit(solution)/shard_map/while/body/eval_jaxpr/scatter-add | solution.py:32
  71.5 2.8 gather_fusion
  74.3 7.4 %fusion.38 = f32[64,128,256]{2,1,0:T(8,128)} fusion(bf16[64,128,256]{2,1,0:T(8,128)(2,1)} %gather_fusion, pred[64]{0:T(512)(128)(4,1)S(1)} %get-tuple-element.178, bf16[256,128,128]{2,1,0:T(8,128)(2,1)} %get-tuple-element.202, s32[]{:T(128)S(6)} %select_n.59), kind=kOutput, calls=%fused_computation.2.clone.1 | convolution fusion | flops 538968064 | bytes 14680132 | tf_op jit(solution)/shard_map/while/body/eval_jaxpr/gab,gbs->gas/dot_general | solution.py:31
  81.7 19.1 %scatter_fusion = f32[32,128,256]{2,1,0:T(8,128)} fusion(f32[32,128,256]{2,1,0:T(8,128)} %get-tuple-element.190, s32[64]{0:T(128)S(1)} %compare_select_fusion.4, f32[64,128,256]{2,1,0:T(8,128)} %fusion.38), kind=kCustom, calls=%fused_computation.1.clone.1 | custom fusion | flops 2097152 | bytes 25166080 | tf_op jit(solution)/shard_map/while/body/eval_jaxpr/scatter-add | solution.py:32
  101.0 2.8 gather_fusion
  103.7 7.4 %fusion.38 = f32[64,128,256]{2,1,0:T(8,128)} fusion(bf16[64,128,256]{2,1,0:T(8,128)(2,1)} %gather_fusion, pred[64]{0:T(512)(128)(4,1)S(1)} %get-tuple-element.178, bf16[256,128,128]{2,1,0:T(8,128)(2,1)} %get-tuple-element.202, s32[]{:T(128)S(6)} %select_n.59), kind=kOutput, calls=%fused_computation.2.clone.1 | convolution fusion | flops 538968064 | bytes 14680132 | tf_op jit(solution)/shard_map/while/body/eval_jaxpr/gab,gbs->gas/dot_general | solution.py:31
  111.2 19.6 %scatter_fusion = f32[32,128,256]{2,1,0:T(8,128)} fusion(f32[32,128,256]{2,1,0:T(8,128)} %get-tuple-element.190, s32[64]{0:T(128)S(1)} %compare_select_fusion.4, f32[64,128,256]{2,1,0:T(8,128)} %fusion.38), kind=kCustom, calls=%fused_computation.1.clone.1 | custom fusion | flops 2097152 | bytes 25166080 | tf_op jit(solution)/shard_map/while/body/eval_jaxpr/scatter-add | solution.py:32
  130.9 2.8 gather_fusion
  133.6 7.4 %fusion.38 = f32[64,128,256]{2,1,0:T(8,128)} fusion(bf16[64,128,256]{2,1,0:T(8,128)(2,1)} %gather_fusion, pred[64]{0:T(512)(128)(4,1)S(1)} %get-tuple-element.178, bf16[256,128,128]{2,1,0:T(8,128)(2,1)} %get-tuple-element.202, s32[]{:T(128)S(6)} %select_n.59), kind=kOutput, calls=%fused_computation.2.clone.1 | convolution fusion | flops 538968064 | bytes 14680132 | tf_op jit(solution)/shard_map/while/body/eval_jaxpr/gab,gbs->gas/dot_general | solution.py:31
  141.1 19.2 %scatter_fusion = f32[32,128,256]{2,1,0:T(8,128)} fusion(f32[32,128,256]{2,1,0:T(8,128)} %get-tuple-element.190, s32[64]{0:T(128)S(1)} %compare_select_fusion.4, f32[64,128,256]{2,1,0:T(8,128)} %fusion.38), kind=kCustom, calls=%fused_computation.1.clone.1 | custom fusion | flops 2097152 | bytes 25166080 | tf_op jit(solution)/shard_map/while/body/eval_jaxpr/scatter-add | solution.py:32
  160.3 50.9 %reduce-scatter.2.cloned.1.call-done = f32[512,256]{1,0:T(8,128)} async-done(((f32[4096,256]{1,0:T(8,128)}), f32[512,256]{1,0:T(8,128)}) %reduce-scatter.2.cloned.1.call-update) | async-done | bytes 524304 | tf_op jit(solution)/shard_map/reduce_scatter | solution.py:52
  211.2 2.3 fusion.11
  213.6 124.0 %all-reduce.4.cloned.1.call-done = f32[128,128]{0,1:T(8,128)} async-done(((f32[128,128]{0,1:T(8,128)}), f32[128,128]{0,1:T(8,128)}) %all-reduce.4.cloned.1.call-update) | async-done | bytes 65552 | tf_op jit(solution)/shard_map/psum | solution.py:57
  337.6 0.8 broadcast_multiply_fusion.2
  338.5 0.1 copy.13
  338.6 0.9 fusion.20
  339.4 11.7 %cholesky.44 = f32[128,128]{1,0:T(8,128)S(1)} custom-call(f32[128,128]{1,0:T(8,128)S(1)} %fusion.20), custom_call_target="Cholesky" | custom-call | tf_op jit(solution)/shard_map/jit(cholesky)/cholesky | solution.py:15
  351.2 0.6 compare_reduce_fusion.1
  351.8 0.7 fusion.22
  352.5 9.8 %custom-call.6 = f32[1,128,128]{1,2,0:T(8,128)S(1)} custom-call(f32[1,128,128]{2,1,0:T(8,128)S(1)} %get-tuple-element.133), custom_call_target="InvertDiagBlocksLowerTriangular" | custom-call | tf_op jit(solution)/shard_map/triangular_solve/custom-call.0 | solution.py:17
  362.3 0.3 fusion.15
  362.6 1.3 fusion.9
  364.0 2.0 fusion.7
  366.0 0.2 all-reduce.6.cloned.1.call-start
  366.2 55.8 %all-gather.6.cloned.1.call-done = f32[4096,128]{1,0:T(8,128)} async-done(((f32[128,128]{1,0:T(8,128)}), f32[4096,128]{1,0:T(8,128)}) %all-gather.6.cloned.1.call-update) | async-done | bytes 2097168 | tf_op jit(solution)/shard_map/all_gather | solution.py:11
  421.9 1.7 reduce_sum.9
  423.7 0.1 copy.14
  423.8 0.6 convolution_subtract_fusion
  424.4 1.2 fusion.24
  425.6 121.0 %all-reduce.6.cloned.1.call-done = f32[128,128]{0,1:T(8,128)} async-done(((f32[128,128]{0,1:T(8,128)}), f32[128,128]{0,1:T(8,128)}) %all-reduce.6.cloned.1.call-update) | async-done | bytes 65552 | tf_op jit(solution)/shard_map/psum | solution.py:64
  546.7 0.8 broadcast_multiply_fusion
  547.5 0.1 copy.16
  547.6 0.9 fusion.18
  548.5 11.7 %cholesky.55 = f32[128,128]{1,0:T(8,128)S(1)} custom-call(f32[128,128]{1,0:T(8,128)S(1)} %fusion.18), custom_call_target="Cholesky" | custom-call | tf_op jit(solution)/shard_map/jit(cholesky)/cholesky | solution.py:15
  560.2 0.6 compare_reduce_fusion
  560.8 0.7 fusion.23
  561.5 0.8 copy.18
  562.4 9.8 %custom-call.7 = f32[1,128,128]{1,2,0:T(8,128)S(1)} custom-call(f32[1,128,128]{2,1,0:T(8,128)S(1)} %get-tuple-element.135), custom_call_target="InvertDiagBlocksLowerTriangular" | custom-call | tf_op jit(solution)/shard_map/triangular_solve/custom-call.0 | solution.py:17
  572.2 0.3 fusion.13
  572.5 0.4 fusion.25
  572.9 1.0 copy.17
  (29 shorter events, 1.0 us)
Async XLA Ops:
  7.2 32.3 %all-gather.4.cloned.1.call-start = ((), (), s32[]{:S(2)}) async-start(), calls=%async_computation.1 | async-start | bytes 1310720 | tf_op jit(solution)/shard_map/all_gather | solution.py:49
  7.9 203.3 %reduce-scatter.2.cloned.1.call-start = ((), (), s32[]{:S(2)}) async-start(), calls=%async_computation.2 | async-start | bytes 4718592 | tf_op jit(solution)/shard_map/reduce_scatter | solution.py:52
  39.5 2.5 copy-start
  160.3 177.4 %all-reduce.4.cloned.1.call-start = ((), (), s32[]{:S(2)}) async-start(), calls=%async_computation.3 | async-start | bytes 131072 | tf_op jit(solution)/shard_map/psum | solution.py:57
  211.2 212.5 %copy-start.1 = (f32[512,256]{1,0:T(8,128)S(1)}, f32[512,256]{1,0:T(8,128)}, u32[]{:S(2)}) copy-start(f32[512,256]{1,0:T(8,128)} %reduce-scatter.2.cloned.1.call-done) | copy-start | bytes 1572868
  213.6 208.4 %all-gather.6.cloned.1.call-start = ((), (), s32[]{:S(2)}) async-start(), calls=%async_computation.5 | async-start | bytes 2162688 | tf_op jit(solution)/shard_map/all_gather | solution.py:11
  366.0 180.7 %all-reduce.6.cloned.1.call-start = ((), (), s32[]{:S(2)}) async-start(), calls=%async_computation.4 | async-start | bytes 131072 | tf_op jit(solution)/shard_map/psum | solution.py:64
Sparse Core Ops, SparseCore 0:
  9.6 29.8 all-gather.3
  160.4 50.7 reduce-scatter.1
  218.3 119.2 all-reduce.3
  366.1 55.8 all-gather.5
  428.9 117.7 all-reduce.5
